TPU v7x, 32 devices: a whole 2x2x4 slice. The times are simulated.
32 devices in a mesh: seq: 4 (over y, x), head: 4 (over z), rep: 2 (over core).
Axes of the slice: x: 2, y: 2, z: 4, core: 2. Of those that a mesh axis runs over, the one named last changes fastest.
Arguments:
- query_heads: bfloat16 [2, 8192, 4096], P('rep', 'seq', 'head'), may hold values from -0.59765625 to 0.59765625
- key_heads: bfloat16 [2, 8192, 4096], P('rep', 'seq', 'head'), may hold values from -0.59765625 to 0.59765625
- value_heads: bfloat16 [2, 8192, 4096], P('rep', 'seq', 'head'), may hold values from -6 to 6
- out_cotangent: bfloat16 [2, 8192, 4096], P('rep', 'seq', 'head'), may hold values from -0.19921875 to 0.19921875
- out_weight: bfloat16 [4096, 4096], P('head'), may hold values from -0.09375 to 0.09375
- doc_ends: int32 [2, 7], P('rep'), may hold values from 1 to 8192, as said below
Outputs:
- grad_query: bfloat16 [2, 8192, 4096], P('rep', 'seq', 'head')
- grad_key: bfloat16 [2, 8192, 4096], P('rep', 'seq', 'head')
- grad_value: bfloat16 [2, 8192, 4096], P('rep', 'seq', 'head')
- grad_weight: float32 [4096, 4096], P('head', ('seq', 'rep'))
Inputs may be any that keep to these rules, and one draw needn't show every extreme that they name: `doc_ends`: each row holds 7 strictly increasing document end offsets; its last entry is 8192.
All inputs are finite; a program needn't handle non-finite values.
Results may differ from a plain program's by a relative error of at most 0.0052.
Values may be sent and summed in bfloat16 or wider, within the bound.
No kernel may reach another device: no remote copies, remote signals or barrier semaphores. Data moves between devices by JAX's collectives and lax.ppermute only.
A program may use at most 320 MiB of HBM per device.

v0:
```python
import jax
import jax.numpy as jnp
from jax import lax
from jax.sharding import PartitionSpec as P

HD = 128
BLOCK = 512
highest = lax.Precision.HIGHEST


def prefix(shard, axis, combine, identity, reverse):
    count, here = (lax.axis_size(axis), lax.axis_index(axis))
    everything = jax.tree.map(lambda part: lax.all_gather(part, axis), shard)
    start = jax.tree.map(
        lambda part, zero: jnp.broadcast_to(jnp.asarray(zero, part.dtype), part.shape),
        shard,
        identity,
    )

    def step(k, before):
        at = count - 1 - k if reverse else k
        reached = at > here if reverse else at < here
        new = combine(before, jax.tree.map(lambda part: part[at], everything))
        return jax.tree.map(lambda a, b: jnp.where(reached, a, b), new, before)

    return lax.fori_loop(0, count, step, start)


def doc_counts(positions, ends_row):
    return jnp.sum((ends_row[None, :] <= positions[:, None]).astype(jnp.int32), axis=1)


def local_pass(queries, keys, values, grads, counts, count_before):
    length, heads, width = queries.shape
    blocks = length // BLOCK
    query_blocks = queries.reshape(blocks, BLOCK, heads, width)
    key_blocks = keys.reshape(blocks, BLOCK, heads, width)
    value_blocks = values.reshape(blocks, BLOCK, heads, width)
    grad_blocks = grads.reshape(blocks, BLOCK, heads, width)
    count_blocks = counts.reshape(blocks, BLOCK)
    before_each = jnp.concatenate([jnp.reshape(count_before, (1,)), count_blocks[:-1, -1]])
    last_each = count_blocks[:, -1]
    rows = lax.broadcasted_iota(jnp.int32, (BLOCK, BLOCK), 0)
    cols = lax.broadcasted_iota(jnp.int32, (BLOCK, BLOCK), 1)
    allowed = (
        (count_blocks[:, :, None] == count_blocks[:, None, :]) & (rows >= cols)[None]
    ).astype(jnp.float32)
    scores = jnp.einsum(
        "nthe,nshe->nhts", query_blocks, key_blocks, preferred_element_type=jnp.float32
    )
    attn = (scores * allowed[:, None]).astype(jnp.bfloat16)
    back = jnp.einsum(
        "nthe,nshe->nhts", grad_blocks, value_blocks, preferred_element_type=jnp.float32
    )
    pgrad = (back * allowed[:, None]).astype(jnp.bfloat16)
    out_intra = jnp.einsum(
        "nhts,nshe->nthe", attn, value_blocks, preferred_element_type=jnp.float32
    )
    dq_intra = jnp.einsum("nhts,nshe->nthe", pgrad, key_blocks, preferred_element_type=jnp.float32)
    dk_intra = jnp.einsum(
        "nhts,nthe->nshe", pgrad, query_blocks, preferred_element_type=jnp.float32
    )
    dv_intra = jnp.einsum("nhts,nthe->nshe", attn, grad_blocks, preferred_element_type=jnp.float32)
    first_match = (count_blocks == before_each[:, None])[:, :, None, None]
    last_match = (count_blocks == last_each[:, None])[:, :, None, None]
    keep = (last_each == before_each).astype(jnp.float32)
    tails = jnp.einsum(
        "nshe,nshf->nhef",
        key_blocks * last_match.astype(jnp.bfloat16),
        value_blocks,
        preferred_element_type=jnp.float32,
    )
    head_sums = jnp.einsum(
        "nthe,nthf->nhef",
        query_blocks * first_match.astype(jnp.bfloat16),
        grad_blocks,
        preferred_element_type=jnp.float32,
    )

    def link_step(state, item):
        return (item[0] + item[1] * state, state)

    empty = jnp.zeros((heads, width, width), jnp.float32)
    final_tail, states_before = lax.scan(link_step, empty, (tails, keep))
    final_head, states_after = lax.scan(link_step, empty, (head_sums, keep), reverse=True)
    first_weight = first_match.astype(jnp.float32)
    last_weight = last_match.astype(jnp.float32)
    outputs = out_intra + first_weight * jnp.einsum(
        "nthe,nhef->nthf", query_blocks.astype(jnp.float32), states_before, precision=highest
    )
    dq = dq_intra + first_weight * jnp.einsum(
        "nthf,nhef->nthe", grad_blocks.astype(jnp.float32), states_before, precision=highest
    )
    dk = dk_intra + last_weight * jnp.einsum(
        "nshf,nhef->nshe", value_blocks.astype(jnp.float32), states_after, precision=highest
    )
    dv = dv_intra + last_weight * jnp.einsum(
        "nshe,nhef->nshf", key_blocks.astype(jnp.float32), states_after, precision=highest
    )
    shape = (length, heads, width)
    return (
        outputs.reshape(shape),
        dq.reshape(shape),
        dk.reshape(shape),
        dv.reshape(shape),
        final_tail,
        final_head,
    )


def link_states(earlier, later):
    return (jnp.maximum(earlier[0], later[0]), later[1] + (1.0 - later[0]) * earlier[1])


def on_device(query_heads, key_heads, value_heads, out_cotangent, out_weight, doc_ends):
    length = query_heads.shape[1]
    heads = query_heads.shape[2] // HD
    queries = query_heads[0].reshape(length, heads, HD)
    keys = key_heads[0].reshape(length, heads, HD)
    values = value_heads[0].reshape(length, heads, HD)
    full_cotangent = lax.all_gather(out_cotangent, "head", axis=2, tiled=True)[0]
    grads_flat = lax.dot_general(
        full_cotangent, out_weight, (((1,), (1,)), ((), ())), preferred_element_type=jnp.float32
    ).astype(jnp.bfloat16)
    grads = grads_flat.reshape(length, heads, HD)
    offset = lax.axis_index("seq") * length
    positions = offset + jnp.arange(length, dtype=jnp.int32)
    ends_row = doc_ends[0]
    counts = doc_counts(positions, ends_row)
    count_before = doc_counts(jnp.reshape(offset - 1, (1,)), ends_row)[0]
    outputs, dq, dk, dv, tail, head = local_pass(queries, keys, values, grads, counts, count_before)
    flag = (counts[-1] != count_before).astype(jnp.float32)
    identity = (jnp.zeros((), jnp.float32), jnp.zeros_like(tail))
    flag_before, carry_before = prefix((flag, tail), "seq", link_states, identity, False)
    flag_after, carry_after = prefix((flag, head), "seq", link_states, identity, True)
    entry_weight = (counts == count_before).astype(jnp.float32)[:, None, None]
    exit_weight = (counts == counts[-1]).astype(jnp.float32)[:, None, None]
    outputs = outputs + entry_weight * jnp.einsum(
        "the,hef->thf", queries.astype(jnp.float32), carry_before, precision=highest
    )
    dq = dq + entry_weight * jnp.einsum(
        "thf,hef->the", grads.astype(jnp.float32), carry_before, precision=highest
    )
    dk = dk + exit_weight * jnp.einsum(
        "thf,hef->the", values.astype(jnp.float32), carry_after, precision=highest
    )
    dv = dv + exit_weight * jnp.einsum(
        "the,hef->thf", keys.astype(jnp.float32), carry_after, precision=highest
    )
    flat = heads * HD
    attention_out = outputs.reshape(length, flat).astype(jnp.bfloat16)
    grad_query = dq.reshape(1, length, flat).astype(jnp.bfloat16)
    grad_key = dk.reshape(1, length, flat).astype(jnp.bfloat16)
    grad_value = dv.reshape(1, length, flat).astype(jnp.bfloat16)
    partial_grad = lax.dot_general(
        attention_out, full_cotangent, (((0,), (0,)), ((), ())), preferred_element_type=jnp.float32
    )
    summed = lax.psum(partial_grad, ("seq", "rep"))
    columns = summed.shape[1] // lax.axis_size(("seq", "rep"))
    grad_weight = lax.dynamic_slice_in_dim(
        summed, lax.axis_index(("seq", "rep")) * columns, columns, 1
    )
    return (grad_query, grad_key, grad_value, grad_weight)


def solution(mesh):
    in_specs = (
        P("rep", "seq", "head"),
        P("rep", "seq", "head"),
        P("rep", "seq", "head"),
        P("rep", "seq", "head"),
        P("head", None),
        P("rep", None),
    )
    out_specs = (
        P("rep", "seq", "head"),
        P("rep", "seq", "head"),
        P("rep", "seq", "head"),
        P("head", ("seq", "rep")),
    )
    return jax.shard_map(
        on_device, mesh=mesh, in_specs=in_specs, out_specs=out_specs, check_vma=False
    )
```

profile of v0, /device:TPU:0, one launch (start us, length us, event | category | flops | bytes accessed | tf_op | source)
XLA Modules:
  0.0 711.5 jit_solution(5314023280602779764)
XLA Ops:
  8.4 5.4 copy.224
  13.8 3.1 copy.225
  16.9 7.6 %copy.175 = bf16[4,512,8,128]{1,3,2,0:T(8,128)(2,1)} copy(bf16[4,512,8,128]{3,2,1,0:T(8,128)(2,1)} %bitcast.142) | data formatting | bytes 8388608 | tf_op jit(solution)/shard_map/reshape;reshape;squeeze | solution.py:37
  25.2 0.8 compare_convert_fusion.2
  26.6 6.2 fusion.15
  33.0 10.0 %while.60 = (s32[]{:T(128)}, f32[8,128,128]{2,1,0:T(8,128)S(1)}, f32[4,8,128,128]{3,2,1,0:T(8,128)S(1)}, f32[4,8,128,128]{3,2,1,0:T(8,128)}, f32[4]{0:T(128)S(1)}, /*index=5*/s32[]{:T(128)}, s32[]{:T(128)}) while((s32[]{:T(128)}, f32[8,128,128]{2,1,0:T(8,128)S(1)}, f32[4,8,128,128]{3,2,1,0:T(8,128)S(1)}, ...), condition=%wide.region_3.4_spmd.clone, body=%wide.region_2.3_spmd.clone.sunk | while | flops 524291 | bytes 2621560 | solution.py:84
  33.7 1.9 bitcast_add_fusion.13
  36.2 1.9 bitcast_add_fusion.13
  38.7 1.9 bitcast_add_fusion.13
  41.2 1.9 bitcast_add_fusion.13
  43.1 0.8 copy-done.1
  48.1 11.7 %all-reduce = f32[4]{0:T(128)S(1)} all-reduce(f32[4]{0:T(128)S(1)} %dynamic-update-slice), channel_id=1, replica_groups=mesh['seq'=4,'head'=4,'rep'=2] {'seq'}, use_global_device_ids=true, to_apply=%add | all-reduce | flops 4 | bytes 32
  59.8 5.3 copy.226
  65.1 7.6 %copy.184 = bf16[4,512,8,128]{1,3,2,0:T(8,128)(2,1)} copy(bf16[4,512,8,128]{3,2,1,0:T(8,128)(2,1)} %bitcast.144) | data formatting | bytes 8388608 | tf_op jit(solution)/shard_map/reshape;reshape;squeeze | solution.py:36
  72.8 2.4 and_convert_fusion
  75.2 11.6 %multiply_convert_fusion = bf16[4,8,512,512]{3,2,1,0:T(8,128)(2,1)} fusion(f32[4,512,512]{2,1,0:T(8,128)} %and_convert_fusion, bf16[4,512,8,128]{1,3,2,0:T(8,128)(2,1)} %copy.184, bf16[4,512,8,128]{1,3,2,0:T(8,128)(2,1)} %copy.175), kind=kOutput, calls=%fused_computation.8 | convolution fusion | flops 2164260864 | bytes 29360128 | tf_op jit(solution)/shard_map/nthe,nshe->nhts/dot_general | solution.py:48
  86.8 17.2 %fusion.24 = f32[4,8,512,128]{3,2,1,0:T(8,128)} fusion(bf16[4,8,512,512]{3,2,1,0:T(8,128)(2,1)} %multiply_convert_fusion, bf16[4,512,8,128]{3,2,1,0:T(8,128)(2,1)} %bitcast.138), kind=kOutput, calls=%fused_computation.39 | convolution fusion | flops 2147483648 | bytes 29360128 | tf_op jit(solution)/shard_map/nhts,nshe->nthe/dot_general | solution.py:56
  104.0 8.4 %bitcast_add_fusion.5 = f32[4,512,8,128]{3,1,2,0:T(8,128)S(1)} fusion(f32[4,8,512,128]{3,2,1,0:T(8,128)} %fusion.24, f32[4,512]{1,0:T(4,128)S(1)} %convert_element_type.133, f32[4,8,128,128]{3,2,1,0:T(8,128)S(1)} %copy-done.4, bf16[4,512,8,128]{1,3,2,0:T(8,128)(2,1)} %copy.184), kind=kOutput, calls=%fused_computation.16 | convolution fusion | flops 3225419776 | bytes 23076864 | tf_op jit(solution)/shard_map/nthe,nhef->nthf/dot_general | solution.py:88
  112.4 8.1 %copy.206 = f32[4,512,8,128]{3,2,1,0:T(8,128)} copy(f32[4,512,8,128]{3,1,2,0:T(8,128)S(1)} %bitcast_add_fusion.5) | data formatting | bytes 16777216 | tf_op jit(solution)/shard_map/add | solution.py:88
  120.5 9.4 %copy.209 = f32[2048,8,128]{0,2,1:T(8,128)} copy(f32[2048,8,128]{2,1,0:T(8,128)} %bitcast.146) | data formatting | bytes 16777216 | tf_op jit(solution)/shard_map/reshape | solution.py:102
  129.8 2.0 compare_convert_fusion
  131.8 11.0 %while.61 = (s32[]{:T(128)}, f32[8,128,128]{2,1,0:T(8,128)S(1)}, s32[]{:T(128)}, f32[4,8,128,128]{3,2,1,0:T(8,128)}, f32[4]{0:T(128)S(1)}, /*index=5*/s32[]{:T(128)}, f32[1]{0:T(128)}, s32[]{:T(128)}) while((s32[]{:T(128)}, f32[8,128,128]{2,1,0:T(8,128)S(1)}, s32[]{:T(128)}, f32[4,8,128,128]{3,2,1,0:T(8,128)}, f32[4]{0:T(128)S(1)}, ...), condition=%wide.region_5.6_spmd.clone, body=%wide.region_4.5_spmd.clone.sunk | while | flops 524293 | bytes 1573009 | solution.py:26
  133.1 1.5 fusion.60
  135.8 1.5 fusion.60
  138.6 1.5 fusion.60
  141.3 1.5 fusion.60
  142.8 10.8 %fusion.6 = bf16[2048,8,128]{0,2,1:T(8,128)(2,1)} fusion(f32[2048,8,128]{0,2,1:T(8,128)} %copy.209, f32[8,128,128]{2,1,0:T(8,128)S(1)} %get-tuple-element.364, bf16[2048,8,128]{2,1,0:T(8,128)(2,1)} %bitcast.145, f32[2048]{0:T(1024)S(1)} %get-tuple-element.507), kind=kOutput, calls=%fused_computation.15 | convolution fusion | flops 3227516928 | bytes 17309696 | tf_op jit(solution)/shard_map/the,hef->thf/dot_general | solution.py:138
  153.6 216.7 %all-gather.6.cloned.1.call-done = bf16[1,2048,4096]{2,1,0:T(8,128)(2,1)} async-done(((bf16[1,2048,1024]{2,1,0:T(8,128)(2,1)}), bf16[1,2048,4096]{2,1,0:T(8,128)(2,1)}) %all-gather.6.cloned.1.call-update) | async-done | bytes 16777232 | tf_op jit(solution)/shard_map/all_gather | solution.py:121
  370.3 24.1 %fusion.17 = bf16[2048,1024]{0,1:T(8,128)(2,1)} fusion(bf16[1024,4096]{1,0:T(8,128)(2,1)} %param.18, bf16[1,2048,4096]{2,1,0:T(8,128)(2,1)} %all-gather.6.cloned.1.call-done), kind=kOutput, calls=%fused_computation.34 | convolution fusion | flops 17181966336 | bytes 29360128 | tf_op jit(solution)/shard_map/dot_general | solution.py:122
  394.4 7.8 %reshape_reshape.3 = bf16[4,512,8,128]{1,0,3,2:T(4,128)(2,1)} reshape(bf16[2048,1024]{0,1:T(8,128)(2,1)} %fusion.17) | data formatting | bytes 8388608 | tf_op jit(solution)/shard_map/reshape;reshape | solution.py:39
  402.2 11.6 %multiply_convert_fusion.1 = bf16[4,8,512,512]{3,2,1,0:T(8,128)(2,1)} fusion(f32[4,512,512]{2,1,0:T(8,128)} %and_convert_fusion, bf16[4,512,8,128]{1,0,3,2:T(4,128)(2,1)} %reshape_reshape.3, bf16[4,512,8,128]{3,2,1,0:T(8,128)(2,1)} %bitcast.139), kind=kOutput, calls=%fused_computation.9 | convolution fusion | flops 2164260864 | bytes 29360128 | tf_op jit(solution)/shard_map/nthe,nshe->nhts/dot_general | solution.py:52
  413.9 14.7 %fusion.34 = f32[4,8,512,128]{3,2,1,0:T(8,128)} fusion(bf16[4,8,512,512]{3,2,1,0:T(8,128)(2,1)} %multiply_convert_fusion.1, bf16[4,512,8,128]{1,3,2,0:T(8,128)(2,1)} %copy.175), kind=kOutput, calls=%fused_computation.62 | convolution fusion | flops 2147483648 | bytes 29360128 | tf_op jit(solution)/shard_map/nhts,nshe->nthe/dot_general | solution.py:59
  428.6 6.5 fusion.13
  435.3 10.6 %while.62 = (s32[]{:T(128)}, f32[8,128,128]{2,1,0:T(8,128)S(1)}, f32[4,8,128,128]{3,2,1,0:T(8,128)S(1)}, f32[4,8,128,128]{3,2,1,0:T(8,128)}, f32[4]{0:T(128)S(1)}, /*index=5*/s32[]{:T(128)}, s32[]{:T(128)}, s32[]{:T(128)}) while((s32[]{:T(128)}, f32[8,128,128]{2,1,0:T(8,128)S(1)}, f32[4,8,128,128]{3,2,1,0:T(8,128)S(1)}, ...), condition=%wide.region_7.8_spmd.clone, body=%wide.region_6.7_spmd.clone.sunk | while | flops 524292 | bytes 2621580 | solution.py:85
  436.1 1.9 bitcast_add_fusion.14
  438.7 1.9 bitcast_add_fusion.14
  441.4 1.9 bitcast_add_fusion.14
  444.0 1.9 bitcast_add_fusion.14
  445.9 0.8 copy-done
  446.8 23.6 %fusion.2 = f32[1024,4096]{1,0:T(8,128)} fusion(bf16[2048,1024]{0,1:T(8,128)(2,1)} %bitcast.157, bf16[1,2048,4096]{2,1,0:T(8,128)(2,1)} %all-gather.6.cloned.1.call-done), kind=kOutput, calls=%fused_computation.10 | convolution fusion | flops 17179869184 | bytes 37748736 | tf_op jit(solution)/shard_map/dot_general | solution.py:155
  470.4 9.9 %bitcast_add_fusion.10 = f32[4,512,8,128]{3,1,2,0:T(8,128)S(1)} fusion(f32[4,8,512,128]{3,2,1,0:T(8,128)} %fusion.34, f32[4,512]{1,0:T(4,128)S(1)} %convert_element_type.133, f32[4,8,128,128]{3,2,1,0:T(8,128)} %copy-done.3, bf16[4,512,8,128]{1,0,3,2:T(4,128)(2,1)} %reshape_reshape.3), kind=kOutput, calls=%fused_computation.24 | convolution fusion | flops 3225419776 | bytes 23076864 | tf_op jit(solution)/shard_map/nthf,nhef->nthe/dot_general | solution.py:91
  480.3 8.1 %copy.179 = f32[4,512,8,128]{3,2,1,0:T(8,128)} copy(f32[4,512,8,128]{3,1,2,0:T(8,128)S(1)} %bitcast_add_fusion.10) | data formatting | bytes 16777216 | tf_op jit(solution)/shard_map/add | solution.py:91
  488.4 9.9 %copy.181 = f32[2048,8,128]{0,2,1:T(8,128)} copy(f32[2048,8,128]{2,1,0:T(8,128)} %bitcast.147) | data formatting | bytes 16777216 | tf_op jit(solution)/shard_map/reshape | solution.py:103
  498.2 10.8 %fusion.9 = bf16[2048,8,128]{0,2,1:T(8,128)(2,1)} fusion(f32[2048,8,128]{0,2,1:T(8,128)} %copy.181, f32[8,128,128]{2,1,0:T(8,128)S(1)} %get-tuple-element.364, bf16[2048,8,128]{0,2,1:T(8,128)(2,1)} %bitcast.150, f32[2048]{0:T(1024)S(1)} %get-tuple-element.507), kind=kOutput, calls=%fused_computation.23 | convolution fusion | flops 3227516928 | bytes 17309696 | tf_op jit(solution)/shard_map/thf,hef->the/dot_general | solution.py:141
  509.0 6.4 copy.210
  515.5 11.9 %fusion.35 = f32[4,8,512,128]{3,2,1,0:T(8,128)} fusion(bf16[4,8,512,512]{3,2,1,0:T(8,128)(2,1)} %multiply_convert_fusion.1, bf16[4,512,8,128]{1,3,2,0:T(8,128)(2,1)} %copy.184), kind=kOutput, calls=%fused_computation.63 | convolution fusion | flops 2147483648 | bytes 29360128 | tf_op jit(solution)/shard_map/nhts,nthe->nshe/dot_general | solution.py:60
  527.3 8.2 %bitcast_add_fusion.8 = f32[4,512,8,128]{3,1,2,0:T(8,128)S(1)} fusion(f32[4,8,512,128]{3,2,1,0:T(8,128)} %fusion.35, f32[4,512]{1,0:T(4,128)S(1)} %copy-done.6, f32[4,8,128,128]{3,2,1,0:T(8,128)S(1)} %get-tuple-element.365, bf16[4,512,8,128]{3,2,1,0:T(8,128)(2,1)} %bitcast.140), kind=kOutput, calls=%fused_computation.21 | convolution fusion | flops 3225419776 | bytes 23076864 | tf_op jit(solution)/shard_map/nshf,nhef->nshe/dot_general | solution.py:94
  535.5 8.1 %copy.188 = f32[4,512,8,128]{3,2,1,0:T(8,128)} copy(f32[4,512,8,128]{3,1,2,0:T(8,128)S(1)} %bitcast_add_fusion.8) | data formatting | bytes 16777216 | tf_op jit(solution)/shard_map/add | solution.py:94
  543.6 9.4 %copy.190 = f32[2048,8,128]{0,2,1:T(8,128)} copy(f32[2048,8,128]{2,1,0:T(8,128)} %bitcast.148) | data formatting | bytes 16777216 | tf_op jit(solution)/shard_map/reshape | solution.py:104
  553.1 7.7 %fusion.36 = f32[4,8,128,512]{2,3,1,0:T(8,128)} fusion(f32[4,8,128,128]{3,2,1,0:T(8,128)S(1)} %get-tuple-element.365, bf16[4,512,8,128]{1,3,2,0:T(8,128)(2,1)} %copy.175), kind=kOutput, calls=%fused_computation.64 | convolution fusion | flops 3221225472 | bytes 14680064 | tf_op jit(solution)/shard_map/nshe,nhef->nshf/dot_general | solution.py:97
  560.7 17.0 %add_bitcast_fusion = f32[4,512,8,128]{3,1,2,0:T(8,128)} fusion(f32[4,8,128,512]{2,3,1,0:T(8,128)} %fusion.36, f32[4,512]{1,0:T(4,128)S(1)} %copy-done.6, bf16[4,8,512,512]{3,2,1,0:T(8,128)(2,1)} %multiply_convert_fusion, bf16[4,512,8,128]{1,0,3,2:T(4,128)(2,1)} %reshape_reshape.3), kind=kOutput, calls=%fused_computation.25 | convolution fusion | flops 2151677952 | bytes 37756928 | tf_op jit(solution)/shard_map/nhts,nthe->nshe/dot_general | solution.py:63
  577.7 11.7 %copy.198 = f32[4,512,8,128]{3,2,1,0:T(8,128)} copy(f32[4,512,8,128]{3,1,2,0:T(8,128)} %add_bitcast_fusion) | data formatting | bytes 16777216 | tf_op jit(solution)/shard_map/add | solution.py:97
  589.4 9.4 %copy.201 = f32[2048,8,128]{0,2,1:T(8,128)} copy(f32[2048,8,128]{2,1,0:T(8,128)} %bitcast.149) | data formatting | bytes 16777216 | tf_op jit(solution)/shard_map/reshape | solution.py:105
  598.9 11.1 %while.63 = (s32[]{:T(128)}, f32[8,128,128]{2,1,0:T(8,128)S(1)}, s32[]{:T(128)}, f32[4,8,128,128]{3,2,1,0:T(8,128)}, f32[4]{0:T(128)S(1)}, /*index=5*/s32[]{:T(128)}, s32[]{:T(128)}, s32[]{:T(128)}, s32[]{:T(128)}, f32[1]{0:T(128)}) while((s32[]{:T(128)}, f32[8,128,128]{2,1,0:T(8,128)S(1)}, s32[]{:T(128)}, ...), condition=%wide.region_9.10_spmd.clone, body=%wide.region_8.9_spmd.clone.sunk | while | flops 524297 | bytes 1573071 | solution.py:26
  600.2 1.5 fusion.61
  603.0 1.5 fusion.61
  605.7 1.5 fusion.61
  608.5 1.5 fusion.61
  610.0 10.9 %fusion.8 = bf16[2048,8,128]{0,2,1:T(8,128)(2,1)} fusion(f32[2048,8,128]{0,2,1:T(8,128)} %copy.190, f32[8,128,128]{2,1,0:T(8,128)S(1)} %get-tuple-element.367, bf16[2048,8,128]{2,1,0:T(8,128)(2,1)} %bitcast.141, f32[2048]{0:T(1024)S(1)} %copy-done.7), kind=kOutput, calls=%fused_computation.20 | convolution fusion | flops 3227516928 | bytes 17309696 | tf_op jit(solution)/shard_map/thf,hef->the/dot_general | solution.py:144
  620.9 6.6 copy.211
  627.5 11.7 %fusion.7 = bf16[2048,8,128]{0,2,1:T(8,128)(2,1)} fusion(f32[2048,8,128]{0,2,1:T(8,128)} %copy.201, f32[8,128,128]{2,1,0:T(8,128)S(1)} %get-tuple-element.367, bf16[2048,8,128]{2,1,0:T(8,128)(2,1)} %bitcast.143, f32[2048]{0:T(1024)S(1)} %copy-done.7), kind=kOutput, calls=%fused_computation.18 | convolution fusion | flops 3227516928 | bytes 17309696 | tf_op jit(solution)/shard_map/the,hef->thf/dot_general | solution.py:147
  639.2 6.4 copy.212
  645.6 56.1 %all-reduce.3.cloned.1.call-done = f32[1024,4096]{1,0:T(8,128)} async-done(((f32[1024,4096]{1,0:T(8,128)}), f32[1024,4096]{1,0:T(8,128)}) %all-reduce.3.cloned.1.call-update) | async-done | bytes 16777232 | tf_op jit(solution)/shard_map/psum | solution.py:158
  701.7 3.1 constant_dynamic-slice_fusion
  (76 shorter events, 16.1 us)
Async XLA Ops:
  7.2 124.7 %all-gather.8.cloned.1.call-start = ((), (), s32[]{:S(2)}) async-start(), calls=%async_computation.2 | async-start | bytes 2621440 | tf_op jit(solution)/shard_map/all_gather | solution.py:13
  8.4 5.4 copy-start.5
  16.9 7.6 %copy-start.8 = (s32[1,7]{1,0:T(1,128)S(1)}, s32[1,7]{1,0:T(1,128)}, u32[]{:S(2)}) copy-start(s32[1,7]{1,0:T(1,128)} %param.19) | copy-start | bytes 88
  43.1 0.8 copy-start.1
  43.1 16.7 %copy-start.3 = (f32[4,8,128,128]{3,2,1,0:T(8,128)}, f32[4,8,128,128]{3,2,1,0:T(8,128)S(1)}, u32[]{:S(2)}) copy-start(f32[4,8,128,128]{3,2,1,0:T(8,128)S(1)} %get-tuple-element.362) | copy-start | bytes 6291460
  43.1 3.7 copy-start.11
  43.9 326.4 %all-gather.6.cloned.1.call-start = ((), (), s32[]{:S(2)}) async-start(), calls=%async_computation | async-start | bytes 20971520 | tf_op jit(solution)/shard_map/all_gather | solution.py:121
  44.6 554.2 %all-gather.10.cloned.1.call-start = ((), (), s32[]{:S(2)}) async-start(), calls=%async_computation.3 | async-start | bytes 2621440 | tf_op jit(solution)/shard_map/all_gather | solution.py:13
  86.8 17.2 %copy-start.4 = (f32[4,8,128,128]{3,2,1,0:T(8,128)S(1)}, f32[4,8,128,128]{3,2,1,0:T(8,128)}, u32[]{:S(2)}) copy-start(f32[4,8,128,128]{3,2,1,0:T(8,128)} %copy-done.3) | copy-start | bytes 6291460
  142.8 10.8 %copy-start.9 = (f32[4]{0:T(128)}, f32[4]{0:T(128)S(1)}, u32[]{:S(2)}) copy-start(f32[4]{0:T(128)S(1)} %get-tuple-element.750) | copy-start | bytes 52
  445.9 0.8 copy-start
  446.7 255.0 %all-reduce.3.cloned.1.call-start = ((), (), s32[]{:S(2)}) async-start(), calls=%async_computation.1 | async-start | bytes 33554432 | tf_op jit(solution)/shard_map/psum | solution.py:158
  515.5 11.9 %copy-start.6 = (f32[4,512]{1,0:T(4,128)S(1)}, f32[4,512]{1,0:T(4,128)}, u32[]{:S(2)}) copy-start(f32[4,512]{1,0:T(4,128)} %get-tuple-element.502) | copy-start | bytes 24580
  589.4 9.5 %copy-start.2 = (f32[8,128,128]{2,1,0:T(8,128)S(1)}, f32[8,128,128]{2,1,0:T(8,128)}, u32[]{:S(2)}) copy-start(f32[8,128,128]{2,1,0:T(8,128)} %custom-call.3) | copy-start | bytes 1572868
  589.4 9.5 %copy-start.10 = (f32[4]{0:T(128)S(1)}, f32[4]{0:T(128)}, u32[]{:S(2)}) copy-start(f32[4]{0:T(128)} %copy-done.9) | copy-start | bytes 52
  598.9 11.1 %copy-start.7 = (f32[2048]{0:T(1024)S(1)}, f32[2048]{0:T(1024)}, u32[]{:S(2)}) copy-start(f32[2048]{0:T(1024)} %get-tuple-element.506) | copy-start | bytes 24580
Sparse Core Ops, SparseCore 0:
  44.0 37.8 all-gather.7
  83.5 286.7 all-gather.5
  446.8 33.3 all-gather.9
  483.9 217.7 all-reduce.2
where the time goes:
time: 718 us; the launch traced here: 712 us
  waiting for transfers between devices  273 us (38%)
  matrix products  223 us (31%)
  local copies, waits for them, and re-layouts  147 us (20%)
  other arithmetic  34.7 us (5%)
  between operations  15.6 us (2%)
  blocking collectives  11.7 us (2%)
    all_gather x1, waiting for transfers between devices, on_device(): lax.all_gather(out_cotangent, 'head', axis=2, tiled=True)[0]  217 us
    psum x1, waiting for transfers between devices, on_device(): summed = lax.psum(partial_grad, ('seq', 'rep'))  56.1 us
    unnamed x33, local copies, waits for them, and re-layouts  36.1 us
    dot_general x1, matrix products, on_device(): lax.dot_general(full_cotangent, out_weight, (((1,), (1,)), ((), ())), pre...  24.1 us
    dot_general x1, matrix products, on_device(): lax.dot_general(attention_out, full_cotangent, (((0,), (0,)), ((), ())),...  23.6 us
    dot_general x1, matrix products, local_pass(): jnp.einsum('nhts,nshe->nthe', attn, value_blocks, preferred_element_type=...  17.2 us
    dot_general x1, matrix products, local_pass(): jnp.einsum('nhts,nthe->nshe', attn, grad_blocks, preferred_element_type=j...  17 us
    add x8, other arithmetic, link_step(): return (item[0] + item[1] * state, state)  15 us
  transfers between devices with their start and end apart: 4, of which 2 were waited for; matrix products, arithmetic and copies ran while one was open for 41% of the time, Pallas kernels for 0%

commit v1 on v0

--- a/solution.py
+++ b/solution.py
@@ -6,6 +6,12 @@
 HD = 128
 BLOCK = 512
 highest = lax.Precision.HIGHEST
+
+
+def gather_by_exchange(x, axis, dim):
+    size = lax.axis_size(axis)
+    repeats = [size if d == dim else 1 for d in range(x.ndim)]
+    return lax.all_to_all(jnp.tile(x, repeats), axis, split_axis=dim, concat_axis=dim, tiled=True)
 
 
 def prefix(shard, axis, combine, identity, reverse):
@@ -118,7 +124,7 @@
     queries = query_heads[0].reshape(length, heads, HD)
     keys = key_heads[0].reshape(length, heads, HD)
     values = value_heads[0].reshape(length, heads, HD)
-    full_cotangent = lax.all_gather(out_cotangent, "head", axis=2, tiled=True)[0]
+    full_cotangent = gather_by_exchange(out_cotangent, "head", 2)[0]
     grads_flat = lax.dot_general(
         full_cotangent, out_weight, (((1,), (1,)), ((), ())), preferred_element_type=jnp.float32
     ).astype(jnp.bfloat16)

time: 718 us -> 977 us (1.36)
  local copies, waits for them, and re-layouts: 147 us -> 312 us
  other arithmetic: 34.7 us -> 132 us
  waiting for transfers between devices: 273 us -> 259 us
    all_to_all x0 -> x1, waiting for transfers between devices: none -> 221 us  [gather_by_exchange(): lax.all_to_all(jnp.tile(x, repeats), axis, split_axis=dim, concat_axis=di...]
    all_gather x1 -> x0, waiting for transfers between devices: 217 us -> none  [on_device(): lax.all_gather(out_cotangent, 'head', axis=2, tiled=True)[0]]
    unnamed x4 -> x5, other arithmetic: 0.01 us -> 99.6 us
    all_to_all x0 -> x1, local copies, waits for them, and re-layouts: none -> 70.4 us  [gather_by_exchange(): lax.all_to_all(jnp.tile(x, repeats), axis, split_axis=dim, concat_axis=di...]
    unnamed x33 -> x44, local copies, waits for them, and re-layouts: 36.1 us -> 90.7 us
    another operation x2 -> x5, local copies, waits for them, and re-layouts: 0.45 us -> 40.9 us  [the longest x3 40.5 us: gather_by_exchange(): jnp.tile(x, repeats)]
    psum x1, waiting for transfers between devices: 56.1 us -> 38.3 us  [on_device(): summed = lax.psum(partial_grad, ('seq', 'rep'))]
  transfers between devices with their start and end apart: 4 -> 4, of which waited for: 2 -> 2; matrix products, arithmetic and copies ran while one was open for 41% -> 35% of each run, Pallas kernels for 0% -> 0%
where the time goes in v1:
time: 977 us; the launch traced here: 966 us
  local copies, waits for them, and re-layouts  312 us (32%)
  waiting for transfers between devices  259 us (27%)
  matrix products  221 us (23%)
  other arithmetic  132 us (14%)
  between operations  15.5 us (2%)
  blocking collectives  11.6 us (1%)
    all_to_all x1, waiting for transfers between devices, gather_by_exchange(): lax.all_to_all(jnp.tile(x, repeats), axis, split_axis=dim, concat_axis=di...  221 us
    unnamed x5, other arithmetic  99.6 us
    unnamed x44, local copies, waits for them, and re-layouts  90.7 us
    all_to_all x1, local copies, waits for them, and re-layouts, gather_by_exchange(): lax.all_to_all(jnp.tile(x, repeats), axis, split_axis=dim, concat_axis=di...  70.4 us
    another operation x3, local copies, waits for them, and re-layouts, gather_by_exchange(): jnp.tile(x, repeats)  40.5 us
    psum x1, waiting for transfers between devices, on_device(): summed = lax.psum(partial_grad, ('seq', 'rep'))  38.3 us
    dot_general x1, matrix products, on_device(): lax.dot_general(full_cotangent, out_weight, (((1,), (1,)), ((), ())), pre...  24.1 us
    dot_general x1, matrix products, on_device(): lax.dot_general(attention_out, full_cotangent, (((0,), (0,)), ((), ())),...  23.4 us
  transfers between devices with their start and end apart: 4, of which 2 were waited for; matrix products, arithmetic and copies ran while one was open for 35% of the time, Pallas kernels for 0%

profile of v1, /device:TPU:0, one launch (start us, length us, event | category | flops | bytes accessed | tf_op | source)
XLA Modules:
  0.0 965.6 jit_solution(17694565220611697482)
XLA Ops:
  7.2 6.4 copy.217
  13.6 4.3 tile.12
  17.9 29.8 %copy.301 = bf16[1,2048,4096]{1,0,2:T(2,128)(2,1)} copy(bf16[1,2048,4096]{1,2,0:T(8,128)(2,1)S(1)} %bitcast.150) | data formatting | bytes 33554432 | tf_op jit(solution)/shard_map/tile | solution.py:14
  48.1 99.6 %reduce.5 = bf16[4096,2048]{1,0:T(8,128)(2,1)} reduce(bf16[4096,1,2048]{2,1,0:T(2,128)(2,1)} %bitcast.143, bf16[]{:T(256)} %broadcast.123), dimensions={1}, to_apply=%bitcast.122.reduce_sub_computation | reduce | bytes 33554432
  147.8 17.0 %reshape.206 = bf16[4,2,1048576]{2,1,0:T(2,128)(2,1)} reshape(bf16[4096,2048]{1,0:T(8,128)(2,1)} %reduce.5) | data formatting | bytes 33554432
  164.8 7.2 all-to-all-start
  172.7 5.3 copy.273
  178.0 7.5 copy.223
  187.3 5.3 copy.272
  192.5 6.2 fusion.15
  198.9 10.0 %while.60 = (s32[]{:T(128)}, f32[8,128,128]{2,1,0:T(8,128)S(1)}, f32[4,8,128,128]{3,2,1,0:T(8,128)S(1)}, f32[4,8,128,128]{3,2,1,0:T(8,128)}, f32[4]{0:T(128)S(1)}, /*index=5*/s32[]{:T(128)}, s32[]{:T(128)}) while((s32[]{:T(128)}, f32[8,128,128]{2,1,0:T(8,128)S(1)}, f32[4,8,128,128]{3,2,1,0:T(8,128)S(1)}, ...), condition=%wide.region_3.4_spmd.clone, body=%wide.region_2.3_spmd.clone.sunk | while | flops 524291 | bytes 2621552 | solution.py:90
  199.6 1.9 bitcast_add_fusion.13
  202.1 1.9 bitcast_add_fusion.13
  204.6 1.9 bitcast_add_fusion.13
  207.1 1.9 bitcast_add_fusion.13
  210.5 5.3 copy.274
  215.8 7.6 copy.232
  226.0 2.4 and_convert_fusion
  228.4 11.5 %multiply_convert_fusion = bf16[4,8,512,512]{3,2,1,0:T(8,128)(2,1)} fusion(f32[4,512,512]{2,1,0:T(8,128)} %and_convert_fusion, bf16[4,512,8,128]{1,3,2,0:T(8,128)(2,1)} %copy.232, bf16[4,512,8,128]{1,3,2,0:T(8,128)(2,1)} %copy.223), kind=kOutput, calls=%fused_computation.8 | convolution fusion | flops 2164260864 | bytes 29360128 | tf_op jit(solution)/shard_map/nthe,nshe->nhts/dot_general | solution.py:54
  239.9 11.6 %all-reduce = f32[4]{0:T(128)S(1)} all-reduce(f32[4]{0:T(128)S(1)} %dynamic-update-slice), channel_id=1, replica_groups=mesh['seq'=4,'head'=4,'rep'=2] {'seq'}, use_global_device_ids=true, to_apply=%add | all-reduce | flops 4 | bytes 32
  251.5 14.7 %fusion.24 = f32[4,8,512,128]{3,2,1,0:T(8,128)} fusion(bf16[4,8,512,512]{3,2,1,0:T(8,128)(2,1)} %multiply_convert_fusion, bf16[4,512,8,128]{3,2,1,0:T(8,128)(2,1)} %bitcast.146), kind=kOutput, calls=%fused_computation.39 | convolution fusion | flops 2147483648 | bytes 29360128 | tf_op jit(solution)/shard_map/nhts,nshe->nthe/dot_general | solution.py:62
  266.2 8.2 bitcast_add_fusion.5
  274.4 8.1 copy.254
  282.5 9.3 copy.257
  291.9 1.8 compare_convert_fusion
  293.6 11.2 %while.61 = (s32[]{:T(128)}, f32[8,128,128]{2,1,0:T(8,128)S(1)}, s32[]{:T(128)}, f32[4,8,128,128]{3,2,1,0:T(8,128)}, f32[4]{0:T(128)S(1)}, /*index=5*/s32[]{:T(128)}, f32[1]{0:T(128)}, s32[]{:T(128)}) while((s32[]{:T(128)}, f32[8,128,128]{2,1,0:T(8,128)S(1)}, s32[]{:T(128)}, f32[4,8,128,128]{3,2,1,0:T(8,128)}, f32[4]{0:T(128)S(1)}, ...), condition=%wide.region_5.6_spmd.clone, body=%wide.region_4.5_spmd.clone.sunk | while | flops 524293 | bytes 1573001 | solution.py:32
  304.8 10.9 %fusion.6 = bf16[2048,8,128]{0,2,1:T(8,128)(2,1)} fusion(f32[2048,8,128]{0,2,1:T(8,128)} %copy.257, f32[8,128,128]{2,1,0:T(8,128)S(1)} %get-tuple-element.364, bf16[2048,8,128]{2,1,0:T(8,128)(2,1)} %bitcast.154, f32[2048]{0:T(1024)S(1)} %get-tuple-element.511), kind=kOutput, calls=%fused_computation.15 | convolution fusion | flops 3227516928 | bytes 17309696 | tf_op jit(solution)/shard_map/the,hef->thf/dot_general | solution.py:144
  315.7 220.7 %all-to-all-done = bf16[4,2,1048576]{2,1,0:T(2,128)(2,1)} async-done(((bf16[4,2,1048576]{2,1,0:T(2,128)(2,1)}), bf16[4,2,1048576]{2,1,0:T(2,128)(2,1)}, u32[]{:S(2)}, u32[]{:S(2)}) %all-to-all-start) | async-done | bytes 16777248 | tf_op jit(solution)/shard_map/all_to_all | solution.py:14
  536.5 35.7 %reshape.207 = bf16[4096,1,2048]{2,1,0:T(2,128)(2,1)} reshape(bf16[4,2,1048576]{2,1,0:T(2,128)(2,1)} %all-to-all-done) | data formatting | bytes 33554432
  572.1 70.4 %copy.219 = bf16[1,2048,4096]{2,1,0:T(8,128)(2,1)} copy(bf16[1,2048,4096]{1,0,2:T(2,128)(2,1)} %bitcast.144) | data formatting | bytes 33554432 | tf_op jit(solution)/shard_map/all_to_all | solution.py:14
  642.5 24.1 %fusion.17 = bf16[2048,1024]{0,1:T(8,128)(2,1)} fusion(bf16[1024,4096]{1,0:T(8,128)(2,1)} %param.18, bf16[1,2048,4096]{2,1,0:T(8,128)(2,1)} %copy.219), kind=kOutput, calls=%fused_computation.34 | convolution fusion | flops 17181966336 | bytes 29360128 | tf_op jit(solution)/shard_map/dot_general | solution.py:128
  666.6 7.8 reshape_reshape.3
  674.4 6.5 fusion.13
  681.2 10.0 %while.62 = (s32[]{:T(128)}, f32[8,128,128]{2,1,0:T(8,128)S(1)}, f32[4,8,128,128]{3,2,1,0:T(8,128)S(1)}, f32[4,8,128,128]{3,2,1,0:T(8,128)}, f32[4]{0:T(128)S(1)}, /*index=5*/s32[]{:T(128)}, s32[]{:T(128)}, s32[]{:T(128)}) while((s32[]{:T(128)}, f32[8,128,128]{2,1,0:T(8,128)S(1)}, f32[4,8,128,128]{3,2,1,0:T(8,128)S(1)}, ...), condition=%wide.region_7.8_spmd.clone, body=%wide.region_6.7_spmd.clone.sunk | while | flops 524292 | bytes 2621572 | solution.py:91
  681.8 1.8 bitcast_add_fusion.14
  684.4 1.8 bitcast_add_fusion.14
  686.9 1.8 bitcast_add_fusion.14
  689.4 1.8 bitcast_add_fusion.14
  691.2 7.9 fusion.36
  699.2 16.5 %add_bitcast_fusion = f32[4,512,8,128]{3,1,2,0:T(8,128)} fusion(f32[4,8,128,512]{2,3,1,0:T(8,128)} %fusion.36, f32[4,512]{1,0:T(4,128)S(1)} %get-tuple-element.506, bf16[4,8,512,512]{3,2,1,0:T(8,128)(2,1)} %multiply_convert_fusion, bf16[4,512,8,128]{1,0,3,2:T(4,128)(2,1)} %reshape_reshape.3), kind=kOutput, calls=%fused_computation.25 | convolution fusion | flops 2151677952 | bytes 37756928 | tf_op jit(solution)/shard_map/nhts,nthe->nshe/dot_general | solution.py:69
  715.7 23.4 %fusion.2 = f32[1024,4096]{1,0:T(8,128)} fusion(bf16[2048,1024]{0,1:T(8,128)(2,1)} %bitcast.167, bf16[1,2048,4096]{2,1,0:T(8,128)(2,1)} %copy.219), kind=kOutput, calls=%fused_computation.10 | convolution fusion | flops 17179869184 | bytes 37748736 | tf_op jit(solution)/shard_map/dot_general | solution.py:161
  739.1 12.0 %multiply_convert_fusion.1 = bf16[4,8,512,512]{3,2,1,0:T(8,128)(2,1)} fusion(f32[4,512,512]{2,1,0:T(8,128)} %and_convert_fusion, bf16[4,512,8,128]{1,0,3,2:T(4,128)(2,1)} %reshape_reshape.3, bf16[4,512,8,128]{3,2,1,0:T(8,128)(2,1)} %bitcast.147), kind=kOutput, calls=%fused_computation.9 | convolution fusion | flops 2164260864 | bytes 29360128 | tf_op jit(solution)/shard_map/nthe,nshe->nhts/dot_general | solution.py:58
  751.1 11.6 %copy.246 = f32[4,512,8,128]{3,2,1,0:T(8,128)} copy(f32[4,512,8,128]{3,1,2,0:T(8,128)} %add_bitcast_fusion) | data formatting | bytes 16777216 | tf_op jit(solution)/shard_map/add | solution.py:103
  762.7 9.6 copy.249
  772.4 11.7 %fusion.35 = f32[4,8,512,128]{3,2,1,0:T(8,128)} fusion(bf16[4,8,512,512]{3,2,1,0:T(8,128)(2,1)} %multiply_convert_fusion.1, bf16[4,512,8,128]{1,3,2,0:T(8,128)(2,1)} %copy.232), kind=kOutput, calls=%fused_computation.64 | convolution fusion | flops 2147483648 | bytes 29360128 | tf_op jit(solution)/shard_map/nhts,nthe->nshe/dot_general | solution.py:66
  784.1 8.1 bitcast_add_fusion.8
  792.2 8.1 copy.236
  800.2 9.4 copy.238
  809.7 15.2 %fusion.34 = f32[4,8,512,128]{3,2,1,0:T(8,128)} fusion(bf16[4,8,512,512]{3,2,1,0:T(8,128)(2,1)} %multiply_convert_fusion.1, bf16[4,512,8,128]{1,3,2,0:T(8,128)(2,1)} %copy.223), kind=kOutput, calls=%fused_computation.63 | convolution fusion | flops 2147483648 | bytes 29360128 | tf_op jit(solution)/shard_map/nhts,nshe->nthe/dot_general | solution.py:65
  824.9 10.5 %bitcast_add_fusion.10 = f32[4,512,8,128]{3,1,2,0:T(8,128)S(1)} fusion(f32[4,8,512,128]{3,2,1,0:T(8,128)} %fusion.34, f32[4,512]{1,0:T(4,128)S(1)} %copy-done.8, f32[4,8,128,128]{3,2,1,0:T(8,128)S(1)} %copy-done.6, bf16[4,512,8,128]{1,0,3,2:T(4,128)(2,1)} %reshape_reshape.3), kind=kOutput, calls=%fused_computation.24 | convolution fusion | flops 3225419776 | bytes 23076864 | tf_op jit(solution)/shard_map/nthf,nhef->nthe/dot_general | solution.py:97
  835.4 8.1 copy.227
  843.5 9.6 copy.229
  853.1 11.1 %fusion.9 = bf16[2048,8,128]{0,2,1:T(8,128)(2,1)} fusion(f32[2048,8,128]{0,2,1:T(8,128)} %copy.229, f32[8,128,128]{2,1,0:T(8,128)S(1)} %copy-done.4, bf16[2048,8,128]{0,2,1:T(8,128)(2,1)} %bitcast.159, f32[2048]{0:T(1024)S(1)} %copy-done.11), kind=kOutput, calls=%fused_computation.23 | convolution fusion | flops 3227516928 | bytes 17309696 | tf_op jit(solution)/shard_map/thf,hef->the/dot_general | solution.py:147
  864.2 6.5 copy.258
  870.7 11.0 %while.63 = (s32[]{:T(128)}, f32[8,128,128]{2,1,0:T(8,128)S(1)}, s32[]{:T(128)}, f32[4,8,128,128]{3,2,1,0:T(8,128)}, f32[4]{0:T(128)S(1)}, /*index=5*/s32[]{:T(128)}, s32[]{:T(128)}, s32[]{:T(128)}, s32[]{:T(128)}, f32[1]{0:T(128)}) while((s32[]{:T(128)}, f32[8,128,128]{2,1,0:T(8,128)S(1)}, s32[]{:T(128)}, ...), condition=%wide.region_9.10_spmd.clone, body=%wide.region_8.9_spmd.clone.sunk | while | flops 524297 | bytes 1573063 | solution.py:32
  872.0 1.5 fusion.61
  874.8 1.5 fusion.61
  880.3 1.5 fusion.61
  881.8 11.8 %fusion.7 = bf16[2048,8,128]{0,2,1:T(8,128)(2,1)} fusion(f32[2048,8,128]{0,2,1:T(8,128)} %copy.249, f32[8,128,128]{2,1,0:T(8,128)S(1)} %get-tuple-element.367, bf16[2048,8,128]{2,1,0:T(8,128)(2,1)} %bitcast.152, f32[2048]{0:T(1024)S(1)} %copy-done.9), kind=kOutput, calls=%fused_computation.18 | convolution fusion | flops 3227516928 | bytes 17309696 | tf_op jit(solution)/shard_map/the,hef->thf/dot_general | solution.py:153
  893.6 6.6 copy.260
  900.2 10.8 %fusion.8 = bf16[2048,8,128]{0,2,1:T(8,128)(2,1)} fusion(f32[2048,8,128]{0,2,1:T(8,128)} %copy.238, f32[8,128,128]{2,1,0:T(8,128)S(1)} %get-tuple-element.367, bf16[2048,8,128]{2,1,0:T(8,128)(2,1)} %bitcast.149, f32[2048]{0:T(1024)S(1)} %copy-done.9), kind=kOutput, calls=%fused_computation.20 | convolution fusion | flops 3227516928 | bytes 17309696 | tf_op jit(solution)/shard_map/thf,hef->the/dot_general | solution.py:150
  910.9 6.5 copy.259
  917.4 38.3 %all-reduce.3.cloned.1.call-done = f32[1024,4096]{1,0:T(8,128)} async-done(((f32[1024,4096]{1,0:T(8,128)}), f32[1024,4096]{1,0:T(8,128)}) %all-reduce.3.cloned.1.call-update) | async-done | bytes 16777232 | tf_op jit(solution)/shard_map/psum | solution.py:164
  955.7 3.1 constant_dynamic-slice_fusion
  (91 shorter events, 23.6 us)
Async XLA Ops:
  164.8 7.8 copy-start.12
  164.8 371.7 %all-to-all-start = ((bf16[4,2,1048576]{2,1,0:T(2,128)(2,1)}), bf16[4,2,1048576]{2,1,0:T(2,128)(2,1)}, u32[]{:S(2)}, u32[]{:S(2)}) async-start(bf16[4,2,1048576]{2,1,0:T(2,128)(2,1)} %reshape.206), calls=%async_computation | async-start | bytes 33554432 | tf_op jit(solution)/shard_map/all_to_all | solution.py:14
  172.0 121.6 %all-gather.5.cloned.1.call-start = ((), (), s32[]{:S(2)}) async-start(), calls=%async_computation.2 | async-start | bytes 2621440 | tf_op jit(solution)/shard_map/all_gather | solution.py:19
  209.0 0.8 copy-start.1
  209.0 57.2 %copy-start.5 = (f32[4,8,128,128]{3,2,1,0:T(8,128)}, f32[4,8,128,128]{3,2,1,0:T(8,128)S(1)}, u32[]{:S(2)}) copy-start(f32[4,8,128,128]{3,2,1,0:T(8,128)S(1)} %get-tuple-element.362) | copy-start | bytes 6291460
  209.8 660.9 %all-gather.7.cloned.1.call-start = ((), (), s32[]{:S(2)}) async-start(), calls=%async_computation.3 | async-start | bytes 2621440 | tf_op jit(solution)/shard_map/all_gather | solution.py:19
  215.8 8.8 copy-start.15
  251.5 14.7 %copy-start.7 = (f32[4,512]{1,0:T(4,128)}, f32[4,512]{1,0:T(4,128)S(1)}, u32[]{:S(2)}) copy-start(f32[4,512]{1,0:T(4,128)S(1)} %convert_element_type.133) | copy-start | bytes 24580
  293.6 22.1 %copy-start.10 = (f32[2048]{0:T(1024)}, f32[2048]{0:T(1024)S(1)}, u32[]{:S(2)}) copy-start(f32[2048]{0:T(1024)S(1)} %get-tuple-element.511) | copy-start | bytes 24580
  304.8 10.9 %copy-start.3 = (f32[8,128,128]{2,1,0:T(8,128)}, f32[8,128,128]{2,1,0:T(8,128)S(1)}, u32[]{:S(2)}) copy-start(f32[8,128,128]{2,1,0:T(8,128)S(1)} %get-tuple-element.364) | copy-start | bytes 1572868
  304.8 10.9 %copy-start.13 = (f32[4]{0:T(128)}, f32[4]{0:T(128)S(1)}, u32[]{:S(2)}) copy-start(f32[4]{0:T(128)S(1)} %get-tuple-element.752) | copy-start | bytes 52
  691.2 7.9 copy-start
  699.1 256.6 %all-reduce.3.cloned.1.call-start = ((), (), s32[]{:S(2)}) async-start(), calls=%async_computation.1 | async-start | bytes 33554432 | tf_op jit(solution)/shard_map/psum | solution.py:164
  809.7 15.2 %copy-start.6 = (f32[4,8,128,128]{3,2,1,0:T(8,128)S(1)}, f32[4,8,128,128]{3,2,1,0:T(8,128)}, u32[]{:S(2)}) copy-start(f32[4,8,128,128]{3,2,1,0:T(8,128)} %copy-done.5) | copy-start | bytes 6291460
  809.7 15.2 %copy-start.8 = (f32[4,512]{1,0:T(4,128)S(1)}, f32[4,512]{1,0:T(4,128)}, u32[]{:S(2)}) copy-start(f32[4,512]{1,0:T(4,128)} %copy-done.7) | copy-start | bytes 24580
  843.5 9.6 copy-start.4
  843.5 9.7 copy-start.11
  864.2 6.5 copy-start.2
  864.2 6.5 copy-start.14
  870.7 11.0 %copy-start.9 = (f32[2048]{0:T(1024)S(1)}, f32[2048]{0:T(1024)}, u32[]{:S(2)}) copy-start(f32[2048]{0:T(1024)} %get-tuple-element.510) | copy-start | bytes 24580
Sparse Core Ops, SparseCore 0:
  209.9 38.1 all-gather.4
  699.3 34.4 all-gather.6
  739.3 216.4 all-reduce.2
